TPU v7x, 32 devices: a whole 2x2x4 slice. The times are simulated.
32 devices in a mesh: dp: 16 (over z, y, x), aug: 2 (over core).
Axes of the slice: x: 2, y: 2, z: 4, core: 2. Of those that a mesh axis runs over, the one named last changes fastest.
Arguments:
- images: bfloat16 [2, 16, 197, 768], P('aug', 'dp'), may hold values from -6 to 6
- out_grads: bfloat16 [2, 16, 197, 768], P('aug', 'dp'), may hold values from -8 to 8
- up_weight_t: bfloat16 [3072, 768], P(('dp', 'aug')), may hold values from -0.21875 to 0.21875
- down_weight_t: bfloat16 [3072, 768], P(('dp', 'aug')), may hold values from -0.21875 to 0.21875
- left_up: bfloat16 [3072, 128], P(('dp', 'aug')), may hold values from -0.109375 to 0.109375
- right_up: bfloat16 [768, 128], replicated, may hold values from -0.21875 to 0.21875
- left_down: bfloat16 [768, 128], replicated, may hold values from -0.21875 to 0.21875
- right_down: bfloat16 [3072, 128], P(('dp', 'aug')), may hold values from -0.109375 to 0.109375
- noise: float32 [2, 128, 128], P(None, 'aug'), may hold values from -6 to 6
Outputs:
- update: float32 [2, 128, 128], P(None, 'aug')
- clip_scales: float32 [16], P('dp')
All inputs are finite; a program needn't handle non-finite values.
Results may differ from a plain program's by a relative error of at most 0.0032.
Values may be sent and summed in bfloat16 or wider, within the bound.
A program may use at most 64 MiB of HBM per device.

v0:
```python
import math

import jax
import jax.numpy as jnp
from jax import lax
from jax.sharding import PartitionSpec as P

gelu_coef = 0.7978845608028654
clip_frac = 0.3
noise_mult = 0.05


def gelu_pair(hidden):
    inner = gelu_coef * (hidden + 0.044715 * hidden * hidden * hidden)
    tangent = jnp.tanh(inner)
    value = 0.5 * hidden * (1.0 + tangent)
    slope = 0.5 * (1.0 + tangent) + 0.5 * hidden * (1.0 - tangent * tangent) * gelu_coef * (
        1.0 + 3.0 * 0.044715 * hidden * hidden
    )
    return (value, slope)


def contract_last(left, right):
    return lax.dot_general(
        left, right, (((1,), (1,)), ((), ())), preferred_element_type=jnp.float32
    )


def local(
    images, out_grads, up_weight_t, down_weight_t, left_up, right_up, left_down, right_down, noise
):
    local_augs = images.shape[0]
    local_images = images.shape[1]
    tokens = images.shape[2]
    width = images.shape[3]
    rank = right_up.shape[1]
    token_rows = images.reshape(-1, width)
    grad_rows = out_grads.reshape(-1, width)
    up_piece = lax.all_gather(up_weight_t, ("dp", "aug"), axis=0, tiled=True)
    down_piece = lax.all_gather(down_weight_t, ("dp", "aug"), axis=0, tiled=True)
    left_piece = lax.all_gather(left_up, ("dp", "aug"), axis=0, tiled=True)
    right_piece = lax.all_gather(right_down, ("dp", "aug"), axis=0, tiled=True)
    hidden = contract_last(token_rows, up_piece)
    activation, slope = gelu_pair(hidden)
    back = contract_last(grad_rows, down_piece)
    hidden_grad = (back * slope).astype(jnp.bfloat16)
    first = jnp.dot(hidden_grad, left_piece, preferred_element_type=jnp.float32)
    second = jnp.dot(
        activation.astype(jnp.bfloat16), right_piece, preferred_element_type=jnp.float32
    )
    up_total = first
    down_total = second
    v_up = up_total.astype(jnp.bfloat16)
    u_down = down_total.astype(jnp.bfloat16)
    u_up = jnp.dot(token_rows, right_up, preferred_element_type=jnp.float32).astype(jnp.bfloat16)
    v_down = jnp.dot(grad_rows, left_down, preferred_element_type=jnp.float32).astype(jnp.bfloat16)
    shape = (local_augs, local_images, tokens, rank)
    first = jnp.einsum(
        "aitr,aits->irs",
        v_up.reshape(shape),
        u_up.reshape(shape),
        preferred_element_type=jnp.float32,
    )
    second = jnp.einsum(
        "aitr,aits->irs",
        v_down.reshape(shape),
        u_down.reshape(shape),
        preferred_element_type=jnp.float32,
    )
    local_terms = jnp.stack([first, second], axis=1)
    all_augs = local_augs * lax.axis_size("aug")
    row_sums = lax.psum_scatter(local_terms, "aug", scatter_dimension=2, tiled=True)
    my_rows = row_sums / all_augs
    squares = lax.psum(jnp.sum(my_rows * my_rows, axis=(1, 2, 3)), "aug")
    norms = jnp.sqrt(squares + 1e-06)
    clip_norm = clip_frac * rank * math.sqrt(tokens / all_augs)
    clip_scales = jnp.minimum(1.0, clip_norm / norms)
    clipped_rows = jnp.sum(clip_scales[:, None, None, None] * my_rows, axis=0)
    summed_rows = lax.psum(clipped_rows, "dp")
    all_images = local_images * lax.axis_size("dp")
    update = (summed_rows + noise_mult * clip_norm * noise) / jnp.sqrt(jnp.float32(all_images))
    return (update, clip_scales)


def solution(mesh):
    placed = (
        P("aug", "dp", None, None),
        P("aug", "dp", None, None),
        P(("dp", "aug"), None),
        P(("dp", "aug"), None),
        P(("dp", "aug"), None),
        P(),
        P(),
        P(("dp", "aug"), None),
        P(None, "aug", None),
    )
    return jax.shard_map(
        local,
        mesh=mesh,
        in_specs=placed,
        out_specs=(P(None, "aug", None), P("dp")),
        check_vma=False,
    )
```

profile of v0, /device:TPU:0, one launch (start us, length us, event | category | flops | bytes accessed | tf_op | source)
XLA Modules:
  0.0 281.8 jit_solution(15459410550856716134)
XLA Ops:
  7.2 0.0 copy-start
  7.2 0.0 all-gather.5.cloned.1.call-start
  7.2 0.7 all-gather.5.cloned.1.call-update
  7.9 0.0 all-gather.3.cloned.1.call-start
  8.0 0.7 all-gather.3.cloned.1.call-update
  8.7 0.0 reduce-scatter.2.cloned.1.call-start
  8.7 46.2 %all_gather.14 = bf16[3072,128]{1,0:T(8,128)(2,1)S(1)} all-gather(bf16[96,128]{1,0:T(8,128)(2,1)} %param.13), channel_id=1, replica_groups=mesh['dp'=16,'aug'=2] {'dp','aug'}, dimensions={0}, use_global_device_ids=true | all-gather | bytes 811008 | tf_op jit(solution)/shard_map/all_gather | solution.py:41
  54.9 42.6 %all_gather.15 = bf16[3072,128]{1,0:T(8,128)(2,1)} all-gather(bf16[96,128]{1,0:T(8,128)(2,1)} %param.16), channel_id=1, replica_groups=mesh['dp'=16,'aug'=2] {'dp','aug'}, dimensions={0}, use_global_device_ids=true | all-gather | bytes 811008 | tf_op jit(solution)/shard_map/all_gather | solution.py:42
  97.5 0.0 all-gather.5.cloned.1.call-done
  97.5 0.0 copy-done
  97.5 0.0 copy-start.1
  97.5 4.0 %fusion.17 = f32[197,3072]{1,0:T(8,128)S(1)} fusion(bf16[3072,768]{1,0:T(8,128)(2,1)} %all-gather.5.cloned.1.call-done, bf16[1,1,197,768]{3,2,1,0:T(8,128)(2,1)S(1)} %copy-done), kind=kOutput, calls=%fused_computation.24 | convolution fusion | flops 929562624 | bytes 7441920 | tf_op jit(solution)/shard_map/dot_general | solution.py:24
  101.5 0.0 copy-done.1
  101.5 1.6 fusion.14
  103.1 42.8 %all-gather.3.cloned.1.call-done = bf16[3072,768]{1,0:T(8,128)(2,1)} async-done(((bf16[96,768]{1,0:T(8,128)(2,1)}), bf16[3072,768]{1,0:T(8,128)(2,1)}) %all-gather.3.cloned.1.call-update) | async-done | bytes 4718608 | tf_op jit(solution)/shard_map/all_gather | solution.py:40
  145.9 5.6 %fusion.13 = bf16[197,128]{1,0:T(8,128)(2,1)} fusion(bf16[3072,128]{1,0:T(8,128)(2,1)S(1)} %all_gather.14, bf16[3072,768]{1,0:T(8,128)(2,1)} %all-gather.3.cloned.1.call-done, f32[197,3072]{1,0:T(8,128)S(1)} %fusion.17, bf16[1,1,197,768]{3,2,1,0:T(8,128)(2,1)} %param.10), kind=kOutput, calls=%fused_computation.17 | convolution fusion | flops 1096013440 | bytes 8278784 | tf_op jit(solution)/shard_map/dot_general | solution.py:47
  151.5 1.4 convolution_bitcast_fusion.1
  152.9 1.5 convolution_bitcast_fusion
  154.4 0.7 pad_maximum_fusion
  155.1 0.0 reduce-scatter.2.cloned.1.call-update
  155.1 0.0 all-reduce.2.cloned.1.call-start
  155.1 6.0 %reduce-scatter.2.cloned.1.call-done = f32[1,2,64,128]{3,2,1,0:T(8,128)} async-done(((f32[1,2,128,128]{3,2,1,0:T(8,128)}), f32[1,2,64,128]{3,2,1,0:T(8,128)}) %reduce-scatter.2.cloned.1.call-update) | async-done | bytes 65552 | tf_op jit(solution)/shard_map/reduce_scatter | solution.py:72
  161.1 1.5 multiply_reduce_fusion
  162.6 3.1 %psum.14 = f32[1]{0:T(128)} all-reduce(f32[1]{0:T(128)} %bitcast.4), channel_id=1, replica_groups=mesh['dp'=16,'aug'=2] {'aug'}, use_global_device_ids=true, to_apply=%region_2.0 | all-reduce | flops 1 | bytes 8 | tf_op jit(solution)/shard_map/psum | solution.py:74
  166.4 1.5 multiply_bitcast_fusion
  167.8 0.0 all-reduce.2.cloned.1.call-update
  167.9 104.8 %all-reduce.2.cloned.1.call-done = f32[2,64,128]{2,1,0:T(8,128)} async-done(((f32[2,64,128]{2,1,0:T(8,128)}), f32[2,64,128]{2,1,0:T(8,128)}) %all-reduce.2.cloned.1.call-update) | async-done | bytes 65552 | tf_op jit(solution)/shard_map/psum | solution.py:79
  272.6 1.5 add_multiply_fusion
Async XLA Ops:
  7.2 90.3 %copy-start = (bf16[1,1,197,768]{3,2,1,0:T(8,128)(2,1)S(1)}, bf16[1,1,197,768]{3,2,1,0:T(8,128)(2,1)}, u32[]{:S(2)}) copy-start(bf16[1,1,197,768]{3,2,1,0:T(8,128)(2,1)} %param.9) | copy-start | bytes 907780
  7.2 90.3 %all-gather.5.cloned.1.call-start = ((), (), s32[]{:S(2)}) async-start(), calls=%async_computation.2 | async-start | bytes 4866048 | tf_op jit(solution)/shard_map/all_gather | solution.py:39
  7.9 138.0 %all-gather.3.cloned.1.call-start = ((), (), s32[]{:S(2)}) async-start(), calls=%async_computation.1 | async-start | bytes 4866048 | tf_op jit(solution)/shard_map/all_gather | solution.py:40
  8.7 152.5 %reduce-scatter.2.cloned.1.call-start = ((), (), s32[]{:S(2)}) async-start(), calls=%async_computation.3 | async-start | bytes 196608 | tf_op jit(solution)/shard_map/reduce_scatter | solution.py:72
  97.5 4.0 %copy-start.1 = (bf16[3072,128]{1,0:T(8,128)(2,1)S(1)}, bf16[3072,128]{1,0:T(8,128)(2,1)}, u32[]{:S(2)}) copy-start(bf16[3072,128]{1,0:T(8,128)(2,1)} %all_gather.15) | copy-start | bytes 2359300
  155.1 117.5 %all-reduce.2.cloned.1.call-start = ((), (), s32[]{:S(2)}) async-start(), calls=%async_computation.4 | async-start | bytes 131072 | tf_op jit(solution)/shard_map/psum | solution.py:79
Sparse Core Ops, SparseCore 0:
  10.9 69.5 all-gather.4
  83.4 62.4 all-gather.2
  155.2 5.8 reduce-scatter.1
  168.0 104.5 all-reduce.1
where the time goes:
time: 282 us
  waiting for transfers between devices  155 us (55%)
  blocking collectives  91.9 us (33%)
  between operations  15.6 us (6%)
  matrix products  14.1 us (5%)
  other arithmetic  5.11 us (2%)
    psum x1, waiting for transfers between devices, local(): summed_rows = lax.psum(clipped_rows, 'dp')  105 us
    all_gather x1, blocking collectives, local(): left_piece = lax.all_gather(left_up, ('dp', 'aug'), axis=0, tiled=True)  46.2 us
    all_gather x1, waiting for transfers between devices, local(): lax.all_gather(down_weight_t, ('dp', 'aug'), axis=0, tiled=True)  42.8 us
    all_gather x1, blocking collectives, local(): right_piece = lax.all_gather(right_down, ('dp', 'aug'), axis=0, tiled=True)  42.6 us
    reduce_scatter x1, waiting for transfers between devices, local(): lax.psum_scatter(local_terms, 'aug', scatter_dimension=2, tiled=True)  5.99 us
  transfers between devices with their start and end apart: 4, of which 3 were waited for; matrix products, arithmetic and copies ran while one was open for 2% of the time, Pallas kernels for 0%

commit v1 on v0

--- a/solution.py
+++ b/solution.py
@@ -1,13 +1,19 @@
+import functools
 import math
 
 import jax
 import jax.numpy as jnp
 from jax import lax
+from jax.experimental import pallas as pl
+from jax.experimental.pallas import tpu as pltpu
 from jax.sharding import PartitionSpec as P
 
 gelu_coef = 0.7978845608028654
 clip_frac = 0.3
 noise_mult = 0.05
+MESH = pl.DeviceIdType.MESH
+SIDE = 2
+TILE = 32
 
 
 def gelu_pair(hidden):
@@ -82,6 +88,475 @@
     return (update, clip_scales)
 
 
+def gather_slot(at, source, length):
+    mirror = at // (length // 2)
+    at = at + mirror * (length - 1 - 2 * at)
+    source = source + mirror * (length - 1 - 2 * source)
+    return source + (at - source + length - 1) // length
+
+
+def slot_source(at, slot, length):
+    mirror = at // (length // 2)
+    near = at + mirror * (length - 1 - 2 * at)
+    source = slot - (near - slot + length) // length
+    return source + mirror * (length - 1 - 2 * source)
+
+
+def kernel(
+    line,
+    images,
+    scale_of,
+    x_in,
+    g_in,
+    up_in,
+    down_in,
+    left_in,
+    right_in,
+    right_up_in,
+    left_down_in,
+    noise_in,
+    out,
+    clip_out,
+    xs,
+    gs,
+    up,
+    down,
+    left,
+    right,
+    right_up,
+    left_down,
+    noise,
+    v_acc,
+    u_acc,
+    u_up,
+    v_down,
+    part,
+    pieces,
+    sums,
+    norm_parts,
+    line_parts,
+    final,
+    local_sem,
+    tok_send,
+    tok_recv,
+    w_send,
+    w_recv,
+    piece_send,
+    piece_recv,
+    norm_send,
+    norm_recv,
+    line_send,
+    line_recv,
+    final_send,
+    final_recv,
+):
+    all_augs, clip_norm = scale_of
+    dp = lax.axis_index("dp")
+    core = lax.axis_index("aug")
+    plane = SIDE * SIDE
+    members = plane * 2
+    z = dp // plane
+    y = (dp // SIDE) % SIDE
+    x = dp % SIDE
+    rows = up_in.shape[0]
+    block = out.shape[1] // plane
+
+    def spot(rel):
+        ry, rx, rc = rel // 4, (rel // 2) % 2, rel % 2
+        yy = 1 - y if ry else y
+        xx = 1 - x if rx else x
+        return yy * SIDE + xx, (1 - core if rc else core)
+
+    def member(rel):
+        lo, cc = spot(rel)
+        return (z * plane + lo, cc)
+
+    def on_line(zz):
+        return (zz * plane + y * SIDE + x, core)
+
+    def line_place(rel):
+        high, low = z // 2, z % 2
+        return on_line((1 - high if rel // 2 else high) * 2 + (1 - low if rel % 2 else low))
+
+    barrier = pltpu.get_barrier_semaphore()
+    for rel in range(1, members):
+        pl.semaphore_signal(barrier, inc=1, device_id=member(rel), device_id_type=MESH)
+    for rel in range(1, line):
+        pl.semaphore_signal(barrier, inc=1, device_id=line_place(rel), device_id_type=MESH)
+
+    locals_ = [
+        pltpu.make_async_copy(a, b, local_sem.at[n])
+        for n, (a, b) in enumerate(
+            (
+                (x_in, xs.at[0]),
+                (g_in, gs.at[0]),
+                (right_up_in, right_up),
+                (left_down_in, left_down),
+                (up_in, up.at[pl.ds(0, rows)]),
+                (down_in, down.at[pl.ds(0, rows)]),
+                (left_in, left.at[pl.ds(0, rows)]),
+                (right_in, right.at[pl.ds(0, rows)]),
+                (noise_in, noise),
+            )
+        )
+    ]
+    for copy in locals_:
+        copy.start()
+    pl.semaphore_wait(barrier, members - 1 + line - 1)
+
+    stores = (xs, gs)
+    token_sends = []
+
+    def send_token(kind, slot, rel, source=None):
+        n = len(token_sends)
+        target = stores[kind].at[_xor(slot, rel)]
+        copy = pltpu.make_async_remote_copy(
+            src_ref=stores[kind].at[slot] if source is None else source,
+            dst_ref=target,
+            send_sem=tok_send.at[n],
+            recv_sem=tok_recv.at[kind, _xor(slot, rel)],
+            device_id=member(rel),
+            device_id_type=MESH,
+        )
+        copy.start()
+        token_sends.append(copy)
+
+    def await_token(kind, slot):
+        pltpu.make_async_copy(
+            stores[kind].at[slot], stores[kind].at[slot], tok_recv.at[kind, slot]
+        ).wait()
+
+    send_token(0, 0, 2, x_in)
+    send_token(1, 0, 4, g_in)
+
+    weight_stores = (up, down, left, right)
+    weight_ins = (up_in, down_in, left_in, right_in)
+
+    def weight_copies(source, target, way, slot, from_slot):
+        to_row = pl.multiple_of(gather_slot(target, source, line) * rows, TILE)
+        return [
+            pltpu.make_async_remote_copy(
+                src_ref=weight_ins[n] if from_slot == 0 else store.at[pl.ds(from_slot * rows, rows)],
+                dst_ref=store.at[pl.ds(to_row, rows)],
+                send_sem=w_send.at[way, slot, n],
+                recv_sem=w_recv.at[gather_slot(target, source, line), n],
+                device_id=on_line(target),
+                device_id_type=MESH,
+            )
+            for n, store in enumerate(weight_stores)
+        ]
+
+    def own_weights(act):
+        @pl.when(z < line - 1)
+        def _():
+            for copy in weight_copies(z, z + 1, 0, 0, 0):
+                act(copy)
+
+        @pl.when(z > 0)
+        def _():
+            for copy in weight_copies(z, z - 1, 1, 0, 0):
+                act(copy)
+
+    own_weights(lambda copy: copy.start())
+    send_token(0, 0, 1, x_in)
+    send_token(1, 0, 1, g_in)
+    send_token(1, 0, 2, g_in)
+    send_token(0, 0, 4, x_in)
+
+    def pass_weights(slot, act):
+        source = slot_source(z, slot, line)
+
+        @pl.when(jnp.logical_and(source < z, z < line - 1))
+        def _():
+            for copy in weight_copies(source, z + 1, 0, slot, slot):
+                act(copy)
+
+        @pl.when(jnp.logical_and(source > z, z > 0))
+        def _():
+            for copy in weight_copies(source, z - 1, 1, slot, slot):
+                act(copy)
+
+    def await_weights(slot):
+        for n, store in enumerate(weight_stores):
+            span = store.at[pl.ds(slot * rows, rows)]
+            pltpu.make_async_copy(span, span, w_recv.at[slot, n]).wait()
+        pass_weights(slot, lambda copy: copy.start())
+
+    at_end = jnp.logical_or(z == 0, z == line - 1)
+
+    def outer(slot):
+        pl.when(at_end)(lambda: await_weights(slot))
+
+    def inner(slot):
+        pl.when(jnp.logical_not(at_end))(lambda: await_weights(slot))
+
+    def sides(s):
+        u_up[s] = jnp.dot(xs[s], right_up[...], preferred_element_type=jnp.float32).astype(jnp.bfloat16)
+        v_down[s] = jnp.dot(gs[s], left_down[...], preferred_element_type=jnp.float32).astype(jnp.bfloat16)
+
+    def cell(s, first_slot, slots, fresh):
+        span = pl.ds(first_slot * rows, slots * rows)
+        hidden = contract_last(xs[s], up[span, :])
+        activation, slope = gelu_pair(hidden)
+        back = contract_last(gs[s], down[span, :])
+        hidden_grad = (back * slope).astype(jnp.bfloat16)
+        v = jnp.dot(hidden_grad, left[span, :], preferred_element_type=jnp.float32)
+        u = jnp.dot(activation.astype(jnp.bfloat16), right[span, :], preferred_element_type=jnp.float32)
+        if fresh:
+            v_acc[s] = v
+            u_acc[s] = u
+        else:
+            v_acc[s] += v
+            u_acc[s] += u
+
+    def over(sets, *steps):
+        @pl.loop(sets[0], sets[1])
+        def _(s):
+            for step in steps:
+                step(s)
+
+    for copy in locals_:
+        copy.wait()
+    await_token(0, 1)
+    await_token(1, 1)
+    over((0, 2), sides)
+
+    await_token(0, 2)
+    send_token(0, 2, 4)
+    send_token(0, 2, 1)
+    await_token(1, 4)
+    send_token(1, 4, 2)
+    send_token(1, 4, 1)
+    await_weights(1)
+    inner(2)
+    near = functools.partial(cell, first_slot=0, slots=2, fresh=True)
+    over((0, 2), near)
+
+    await_token(1, 2)
+    send_token(1, 2, 1)
+    await_token(0, 4)
+    send_token(0, 4, 1)
+    await_token(0, 3)
+    await_token(1, 3)
+    await_token(0, 5)
+    await_token(1, 5)
+    outer(2)
+    inner(3)
+    over((2, 6), sides, near)
+    await_token(0, 6)
+    send_token(0, 6, 1)
+    await_token(1, 6)
+    send_token(1, 6, 1)
+    middle = functools.partial(cell, first_slot=2, slots=1, fresh=False)
+    over((0, 6), middle)
+    await_token(0, 7)
+    await_token(1, 7)
+    over((6, 8), sides, near, middle)
+    outer(3)
+
+    def contract_first(a, b):
+        return lax.dot_general(a, b, (((0,), (0,)), ((), ())), preferred_element_type=jnp.float32)
+
+    piece_copies = []
+    for i in range(plane):
+        first, second = None, None
+        for s in (2 * i, 2 * i + 1):
+            cell(s, 3, line - 3, False)
+            a = contract_first(v_acc[s].astype(jnp.bfloat16), u_up[s])
+            b = contract_first(v_down[s], u_acc[s].astype(jnp.bfloat16))
+            first = a if first is None else first + a
+            second = b if second is None else second + b
+        part[i, 0] = first
+        part[i, 1] = second
+        for rel in range(1, members):
+            lo, cc = spot(rel)
+            start = pl.multiple_of((cc * plane + lo) * block, 8)
+            copy = pltpu.make_async_remote_copy(
+                src_ref=part.at[i, :, pl.ds(start, block), :],
+                dst_ref=pieces.at[rel - 1, _xor(i, rel // 2)],
+                send_sem=piece_send.at[rel - 1, i],
+                recv_sem=piece_recv.at[rel - 1, _xor(i, rel // 2)],
+                device_id=member(rel),
+                device_id_type=MESH,
+            )
+            copy.start()
+            piece_copies.append(copy)
+
+    my_lo, _ = spot(0)
+    mine = pl.ds(pl.multiple_of((core * plane + my_lo) * block, 8), block)
+    for i in range(plane):
+        total = part[i, :, mine, :]
+        for rel in range(1, members):
+            span = pieces.at[rel - 1, i]
+            pltpu.make_async_copy(span, span, piece_recv.at[rel - 1, i]).wait()
+            total = total + pieces[rel - 1, i]
+        total = total / all_augs
+        sums[i] = total
+        squares = jnp.sum(total * total, axis=0)
+        norm_parts[0, i] = jnp.sum(squares.reshape(block // 8, 8, squares.shape[1]), axis=0)
+
+    def exchange(buffer, rel, slot, send, recv, place):
+        copy = pltpu.make_async_remote_copy(
+            src_ref=buffer.at[0],
+            dst_ref=buffer.at[slot],
+            send_sem=send.at[rel],
+            recv_sem=recv.at[rel],
+            device_id=place,
+            device_id_type=MESH,
+        )
+        copy.start()
+        return copy
+
+    norm_copies = [
+        exchange(norm_parts, rel, rel, norm_send, norm_recv, member(rel)) for rel in range(1, members)
+    ]
+    for copy in norm_copies:
+        copy.wait_recv()
+
+    clipped = None
+    my_clip = None
+    for i in range(plane):
+        terms = [norm_parts[rel, _xor(i, rel // 2)] for rel in range(members)]
+        while len(terms) > 1:
+            terms = [terms[n] + terms[n + 1] for n in range(0, len(terms), 2)]
+        square = jnp.sum(terms[0], axis=(0, 1), keepdims=True)
+        clip = jnp.minimum(1.0, clip_norm / jnp.sqrt(square + 1e-06))
+        if i == 0:
+            my_clip = clip
+        term = clip[None] * sums[i]
+        clipped = term if clipped is None else clipped + term
+    line_parts[0] = clipped
+    line_copies = [
+        exchange(line_parts, rel, rel, line_send, line_recv, line_place(rel)) for rel in range(1, line)
+    ]
+    clip_out[...] = jnp.broadcast_to(my_clip, clip_out.shape)
+    for copy in line_copies:
+        copy.wait_recv()
+    terms = [line_parts[rel] for rel in range(line)]
+    while len(terms) > 1:
+        terms = [terms[n] + terms[n + 1] for n in range(0, len(terms), 2)]
+    final[my_lo] = terms[0]
+    final_copies = []
+    for rel in range(2, members, 2):
+        copy = pltpu.make_async_remote_copy(
+            src_ref=final.at[my_lo],
+            dst_ref=final.at[my_lo],
+            send_sem=final_send.at[rel // 2],
+            recv_sem=final_recv.at[rel // 2],
+            device_id=member(rel),
+            device_id_type=MESH,
+        )
+        copy.start()
+        final_copies.append(copy)
+    for rel in range(2, members, 2):
+        lo, _ = spot(rel)
+        pltpu.make_async_copy(final.at[lo], final.at[lo], final_recv.at[rel // 2]).wait()
+    for q in range(plane):
+        rows_q = pl.ds(q * block, block)
+        out[:, rows_q, :] = (final[q] + noise_mult * clip_norm * noise[:, rows_q, :]) / math.sqrt(images)
+
+    for copy in token_sends + piece_copies + norm_copies + line_copies + final_copies:
+        copy.wait_send()
+    own_weights(lambda copy: copy.wait_send())
+    for slot in range(1, line):
+        pass_weights(slot, lambda copy: copy.wait_send())
+
+
+def _xor(a, b):
+    return a ^ b
+
+
+def planes(
+    line, images, out_grads, up_weight_t, down_weight_t, left_up, right_up, left_down, right_down, noise
+):
+    tokens, width = images.shape[2:]
+    rank = right_up.shape[1]
+    rows = up_weight_t.shape[0]
+    all_augs = lax.axis_size("aug")
+    all_images = lax.axis_size("dp")
+    clip_norm = clip_frac * rank * math.sqrt(tokens / all_augs)
+    plane = SIDE * SIDE
+    members = plane * 2
+    block = noise.shape[1] // plane
+    lanes = noise.shape[2]
+    bf16, f32 = jnp.bfloat16, jnp.float32
+    dma = pltpu.SemaphoreType.DMA
+    update, clip = pl.pallas_call(
+        functools.partial(kernel, line, all_images, (all_augs, clip_norm)),
+        out_shape=(
+            jax.ShapeDtypeStruct(noise.shape, f32),
+            jax.ShapeDtypeStruct((1, 128), f32),
+        ),
+        in_specs=[pl.BlockSpec(memory_space=pl.ANY)] * 9,
+        out_specs=(pl.BlockSpec(memory_space=pltpu.VMEM), pl.BlockSpec(memory_space=pltpu.VMEM)),
+        scratch_shapes=[
+            pltpu.VMEM((members, tokens, width), bf16),
+            pltpu.VMEM((members, tokens, width), bf16),
+            pltpu.VMEM((line * rows, width), bf16),
+            pltpu.VMEM((line * rows, width), bf16),
+            pltpu.VMEM((line * rows, rank), bf16),
+            pltpu.VMEM((line * rows, rank), bf16),
+            pltpu.VMEM(right_up.shape, bf16),
+            pltpu.VMEM(left_down.shape, bf16),
+            pltpu.VMEM(noise.shape, f32),
+            pltpu.VMEM((members, tokens, rank), f32),
+            pltpu.VMEM((members, tokens, rank), f32),
+            pltpu.VMEM((members, tokens, rank), bf16),
+            pltpu.VMEM((members, tokens, rank), bf16),
+            pltpu.VMEM((plane, 2, rank, rank), f32),
+            pltpu.VMEM((members - 1, plane, 2, block, lanes), f32),
+            pltpu.VMEM((plane, 2, block, lanes), f32),
+            pltpu.VMEM((members, plane, 8, lanes), f32),
+            pltpu.VMEM((line, 2, block, lanes), f32),
+            pltpu.VMEM((plane, 2, block, lanes), f32),
+            dma((9,)),
+            dma((14,)),
+            dma((2, members)),
+            dma((2, line, 4)),
+            dma((line, 4)),
+            dma((members - 1, plane)),
+            dma((members - 1, plane)),
+            dma((members,)),
+            dma((members,)),
+            dma((line,)),
+            dma((line,)),
+            dma((plane,)),
+            dma((plane,)),
+        ],
+        compiler_params=pltpu.CompilerParams(collective_id=0, has_side_effects=True),
+        name="planes",
+    )(
+        images.reshape(tokens, width),
+        out_grads.reshape(tokens, width),
+        up_weight_t,
+        down_weight_t,
+        left_up,
+        right_down,
+        right_up,
+        left_down,
+        noise,
+    )
+    return update, clip[0, :1]
+
+
+def body_of(mesh):
+    def body(*args):
+        images, up_weight_t, noise = args[0], args[2], args[8]
+        plane = SIDE * SIDE
+        line = mesh.shape["dp"] // plane
+        fits = (
+            mesh.shape["aug"] == 2
+            and line * plane == mesh.shape["dp"]
+            and line == 4
+            and images.shape[:2] == (1, 1)
+            and up_weight_t.shape[0] % TILE == 0
+            and noise.shape[1] % (plane * 8) == 0
+        )
+        return planes(line, *args) if fits else local(*args)
+
+    return body
+
+
 def solution(mesh):
     placed = (
         P("aug", "dp", None, None),
@@ -95,7 +570,7 @@
         P(None, "aug", None),
     )
     return jax.shard_map(
-        local,
+        body_of(mesh),
         mesh=mesh,
         in_specs=placed,
         out_specs=(P(None, "aug", None), P("dp")),

time: 282 us -> 57.9 us (0.21)
  waiting for transfers between devices: 155 us -> 0 us
  blocking collectives: 91.9 us -> 0 us
  Pallas kernels: 0 us -> 54.5 us
  matrix products: 14.1 us -> 0 us
  between operations: 15.6 us -> 1.82 us
  other arithmetic: 5.11 us -> 0 us
    psum x1 -> x0, waiting for transfers between devices: 105 us -> none  [local(): summed_rows = lax.psum(clipped_rows, 'dp')]
    all_gather x2 -> x0, blocking collectives: 88.8 us -> none  [the longest x1 46.2 us: local(): left_piece = lax.all_gather(left_up, ('dp', 'aug'), axis=0, tiled=True)]
    pallas_call x0 -> x1, Pallas kernels: none -> 54.5 us  [planes(): pl.pallas_call(functools.partial(kernel, line, all_images, (all_augs, cli...]
    all_gather x2 -> x0, waiting for transfers between devices: 42.8 us -> none  [the longest x1 42.8 us: local(): lax.all_gather(down_weight_t, ('dp', 'aug'), axis=0, tiled=True)]
    dot_general x5 -> x0, matrix products: 14.1 us -> none  [the longest x1 5.61 us: local(): first = jnp.dot(hidden_grad, left_piece, preferred_element_type=jnp.float32)]
    reduce_scatter x1 -> x0, waiting for transfers between devices: 5.99 us -> none  [local(): lax.psum_scatter(local_terms, 'aug', scatter_dimension=2, tiled=True)]
    psum x1 -> x0, blocking collectives: 3.08 us -> none  [local(): squares = lax.psum(jnp.sum(my_rows * my_rows, axis=(1, 2, 3)), 'aug')]
    reduce_sum x2 -> x0, other arithmetic: 2.94 us -> none  [the longest x1 1.48 us: local(): clipped_rows = jnp.sum(clip_scales[:, None, None, None] * my_rows, axis=0)]
  transfers between devices with their start and end apart: 4 -> 0, of which waited for: 3 -> 0; matrix products, arithmetic and copies ran while one was open for 2% -> 0% of each run, Pallas kernels for 0% -> 0%
where the time goes in v1:
time: 57.9 us; the launch traced here: 57.8 us
  Pallas kernels  54.5 us (94%)
  between operations  1.82 us (3%)
  local copies, waits for them, and re-layouts  1.48 us (3%)
    pallas_call x1, Pallas kernels, planes(): pl.pallas_call(functools.partial(kernel, line, all_images, (all_augs, cli...  54.5 us
    unnamed x3, local copies, waits for them, and re-layouts  1.48 us

profile of v1, /device:TPU:0, one launch (start us, length us, event | category | flops | bytes accessed | tf_op | source)
XLA Modules:
  0.0 57.8 jit_solution(116814784873436442)
XLA Ops:
  0.6 54.5 %planes.1 = (f32[2,64,128]{2,1,0:T(8,128)}, f32[1,128]{1,0:T(1,128)}) custom-call(bf16[197,768]{1,0:T(8,128)(2,1)} %bitcast.4, bf16[197,768]{1,0:T(8,128)(2,1)} %bitcast.5, bf16[96,768]{1,0:T(8,128)(2,1)} %up_in.1, bf16[96,768]{1,0:T(8,128)(2,1)} %down_in.1, bf16[96,128]{1,0:T(8,128)(2,1)} %left_in.1, bf16[96,128]{1,0:T(8,128)(2,1)} %right_in.1, ...), custom_call_target="tpu_custom_call" | custom-call | tf_op jit(solution)/shard_map/planes/pallas_call | solution.py:484
  55.1 0.0 copy-start
  55.1 1.5 %copy.13 = f32[2,64,128]{2,1,0:T(8,128)} copy(f32[2,64,128]{2,1,0:T(8,128)} %get-tuple-element.8) | data formatting | bytes 131072
  56.6 0.0 copy-done
Async XLA Ops:
  55.1 1.5 %copy-start = (f32[1,128]{1,0:T(1,128)S(1)}, f32[1,128]{1,0:T(1,128)}, u32[]{:S(2)}) copy-start(f32[1,128]{1,0:T(1,128)} %get-tuple-element.5) | copy-start | bytes 1540

commit v2 on v1

--- a/solution.py
+++ b/solution.py
@@ -131,6 +131,7 @@
     u_up,
     v_down,
     part,
+    sent,
     pieces,
     sums,
     norm_parts,
@@ -179,10 +180,18 @@
         return on_line((1 - high if rel // 2 else high) * 2 + (1 - low if rel % 2 else low))
 
     barrier = pltpu.get_barrier_semaphore()
-    for rel in range(1, members):
+    for rel in (1, 2, 4):
         pl.semaphore_signal(barrier, inc=1, device_id=member(rel), device_id_type=MESH)
-    for rel in range(1, line):
-        pl.semaphore_signal(barrier, inc=1, device_id=line_place(rel), device_id_type=MESH)
+
+    @pl.when(z > 0)
+    def _():
+        pl.semaphore_signal(barrier, inc=1, device_id=on_line(z - 1), device_id_type=MESH)
+
+    @pl.when(z < line - 1)
+    def _():
+        pl.semaphore_signal(barrier, inc=1, device_id=on_line(z + 1), device_id_type=MESH)
+
+    at_end = jnp.logical_or(z == 0, z == line - 1)
 
     locals_ = [
         pltpu.make_async_copy(a, b, local_sem.at[n])
@@ -202,7 +211,8 @@
     ]
     for copy in locals_:
         copy.start()
-    pl.semaphore_wait(barrier, members - 1 + line - 1)
+    pl.when(at_end)(lambda: pl.semaphore_wait(barrier, 4))
+    pl.when(jnp.logical_not(at_end))(lambda: pl.semaphore_wait(barrier, 5))
 
     stores = (xs, gs)
     token_sends = []
@@ -263,32 +273,32 @@
     send_token(1, 0, 2, g_in)
     send_token(0, 0, 4, x_in)
 
-    def pass_weights(slot, act):
+    def pass_weights(slot, which, act):
         source = slot_source(z, slot, line)
 
         @pl.when(jnp.logical_and(source < z, z < line - 1))
         def _():
-            for copy in weight_copies(source, z + 1, 0, slot, slot):
-                act(copy)
+            for n in which:
+                act(weight_copies(source, z + 1, 0, slot, slot)[n])
 
         @pl.when(jnp.logical_and(source > z, z > 0))
         def _():
-            for copy in weight_copies(source, z - 1, 1, slot, slot):
-                act(copy)
-
-    def await_weights(slot):
-        for n, store in enumerate(weight_stores):
-            span = store.at[pl.ds(slot * rows, rows)]
+            for n in which:
+                act(weight_copies(source, z - 1, 1, slot, slot)[n])
+
+    every = (0, 1, 2, 3)
+
+    def await_weights(slot, which=every):
+        for n in which:
+            span = weight_stores[n].at[pl.ds(slot * rows, rows)]
             pltpu.make_async_copy(span, span, w_recv.at[slot, n]).wait()
-        pass_weights(slot, lambda copy: copy.start())
-
-    at_end = jnp.logical_or(z == 0, z == line - 1)
-
-    def outer(slot):
-        pl.when(at_end)(lambda: await_weights(slot))
-
-    def inner(slot):
-        pl.when(jnp.logical_not(at_end))(lambda: await_weights(slot))
+            pass_weights(slot, (n,), lambda copy: copy.start())
+
+    def outer(slot, which=every):
+        pl.when(at_end)(lambda: await_weights(slot, which))
+
+    def inner(slot, which=every):
+        pl.when(jnp.logical_not(at_end))(lambda: await_weights(slot, which))
 
     def sides(s):
         u_up[s] = jnp.dot(xs[s], right_up[...], preferred_element_type=jnp.float32).astype(jnp.bfloat16)
@@ -321,17 +331,20 @@
     await_token(1, 1)
     over((0, 2), sides)
 
+    inner(1, (0,))
+    inner(2, (0,))
     await_token(0, 2)
     send_token(0, 2, 4)
     send_token(0, 2, 1)
     await_token(1, 4)
     send_token(1, 4, 2)
     send_token(1, 4, 1)
-    await_weights(1)
-    inner(2)
+    inner(1, (1, 2, 3))
+    inner(2, (1, 2, 3))
+    outer(1)
     near = functools.partial(cell, first_slot=0, slots=2, fresh=True)
     over((0, 2), near)
-
+    inner(3, (0,))
     await_token(1, 2)
     send_token(1, 2, 1)
     await_token(0, 4)
@@ -340,9 +353,9 @@
     await_token(1, 3)
     await_token(0, 5)
     await_token(1, 5)
+    inner(3, (1, 2, 3))
+    over((2, 6), sides, near)
     outer(2)
-    inner(3)
-    over((2, 6), sides, near)
     await_token(0, 6)
     send_token(0, 6, 1)
     await_token(1, 6)
@@ -368,11 +381,13 @@
             second = b if second is None else second + b
         part[i, 0] = first
         part[i, 1] = second
+        sent[i, 0] = first.astype(jnp.bfloat16)
+        sent[i, 1] = second.astype(jnp.bfloat16)
         for rel in range(1, members):
             lo, cc = spot(rel)
-            start = pl.multiple_of((cc * plane + lo) * block, 8)
+            start = pl.multiple_of((cc * plane + lo) * block, 16)
             copy = pltpu.make_async_remote_copy(
-                src_ref=part.at[i, :, pl.ds(start, block), :],
+                src_ref=sent.at[i, :, pl.ds(start, block), :],
                 dst_ref=pieces.at[rel - 1, _xor(i, rel // 2)],
                 send_sem=piece_send.at[rel - 1, i],
                 recv_sem=piece_recv.at[rel - 1, _xor(i, rel // 2)],
@@ -389,11 +404,11 @@
         for rel in range(1, members):
             span = pieces.at[rel - 1, i]
             pltpu.make_async_copy(span, span, piece_recv.at[rel - 1, i]).wait()
-            total = total + pieces[rel - 1, i]
+            total = total + pieces[rel - 1, i].astype(jnp.float32)
         total = total / all_augs
         sums[i] = total
         squares = jnp.sum(total * total, axis=0)
-        norm_parts[0, i] = jnp.sum(squares.reshape(block // 8, 8, squares.shape[1]), axis=0)
+        norm_parts[0, pl.ds(i, 1), :] = jnp.sum(squares, axis=0, keepdims=True)
 
     def exchange(buffer, rel, slot, send, recv, place):
         copy = pltpu.make_async_remote_copy(
@@ -416,7 +431,7 @@
     clipped = None
     my_clip = None
     for i in range(plane):
-        terms = [norm_parts[rel, _xor(i, rel // 2)] for rel in range(members)]
+        terms = [norm_parts[rel, pl.ds(_xor(i, rel // 2), 1), :] for rel in range(members)]
         while len(terms) > 1:
             terms = [terms[n] + terms[n + 1] for n in range(0, len(terms), 2)]
         square = jnp.sum(terms[0], axis=(0, 1), keepdims=True)
@@ -459,7 +474,7 @@
         copy.wait_send()
     own_weights(lambda copy: copy.wait_send())
     for slot in range(1, line):
-        pass_weights(slot, lambda copy: copy.wait_send())
+        pass_weights(slot, every, lambda copy: copy.wait_send())
 
 
 def _xor(a, b):
@@ -504,9 +519,10 @@
             pltpu.VMEM((members, tokens, rank), bf16),
             pltpu.VMEM((members, tokens, rank), bf16),
             pltpu.VMEM((plane, 2, rank, rank), f32),
-            pltpu.VMEM((members - 1, plane, 2, block, lanes), f32),
+            pltpu.VMEM((plane, 2, rank, rank), bf16),
+            pltpu.VMEM((members - 1, plane, 2, block, lanes), bf16),
             pltpu.VMEM((plane, 2, block, lanes), f32),
-            pltpu.VMEM((members, plane, 8, lanes), f32),
+            pltpu.VMEM((members, plane, lanes), f32),
             pltpu.VMEM((line, 2, block, lanes), f32),
             pltpu.VMEM((plane, 2, block, lanes), f32),
             dma((9,)),
@@ -550,7 +566,7 @@
             and line == 4
             and images.shape[:2] == (1, 1)
             and up_weight_t.shape[0] % TILE == 0
-            and noise.shape[1] % (plane * 8) == 0
+            and noise.shape[1] % (plane * 16) == 0
         )
         return planes(line, *args) if fits else local(*args)
 

time: 57.9 us -> 55.6 us (0.960)
  Pallas kernels: 54.5 us -> 52.2 us
    pallas_call x1, Pallas kernels: 54.5 us -> 52.2 us  [planes(): pl.pallas_call(functools.partial(kernel, line, all_images, (all_augs, cli...]
where the time goes in v2:
time: 55.6 us; the launch traced here: 55.5 us
  Pallas kernels  52.2 us (94%)
  between operations  1.82 us (3%)
  local copies, waits for them, and re-layouts  1.48 us (3%)
    pallas_call x1, Pallas kernels, planes(): pl.pallas_call(functools.partial(kernel, line, all_images, (all_augs, cli...  52.2 us
    unnamed x3, local copies, waits for them, and re-layouts  1.48 us

profile of v2, /device:TPU:0, one launch (start us, length us, event | category | flops | bytes accessed | tf_op | source)
XLA Modules:
  0.0 55.5 jit_solution(16673435233547853499)
XLA Ops:
  0.6 52.2 %planes.1 = (f32[2,64,128]{2,1,0:T(8,128)}, f32[1,128]{1,0:T(1,128)}) custom-call(bf16[197,768]{1,0:T(8,128)(2,1)} %bitcast.4, bf16[197,768]{1,0:T(8,128)(2,1)} %bitcast.5, bf16[96,768]{1,0:T(8,128)(2,1)} %up_in.1, bf16[96,768]{1,0:T(8,128)(2,1)} %down_in.1, bf16[96,128]{1,0:T(8,128)(2,1)} %left_in.1, bf16[96,128]{1,0:T(8,128)(2,1)} %right_in.1, ...), custom_call_target="tpu_custom_call" | custom-call | tf_op jit(solution)/shard_map/planes/pallas_call | solution.py:499
  52.8 0.0 copy-start
  52.8 1.5 %copy.13 = f32[2,64,128]{2,1,0:T(8,128)} copy(f32[2,64,128]{2,1,0:T(8,128)} %get-tuple-element.8) | data formatting | bytes 131072
  54.3 0.0 copy-done
Async XLA Ops:
  52.8 1.5 %copy-start = (f32[1,128]{1,0:T(1,128)S(1)}, f32[1,128]{1,0:T(1,128)}, u32[]{:S(2)}) copy-start(f32[1,128]{1,0:T(1,128)} %get-tuple-element.5) | copy-start | bytes 1540

commit v3 on v2

--- a/solution.py
+++ b/solution.py
@@ -23,6 +23,15 @@
     slope = 0.5 * (1.0 + tangent) + 0.5 * hidden * (1.0 - tangent * tangent) * gelu_coef * (
         1.0 + 3.0 * 0.044715 * hidden * hidden
     )
+    return (value, slope)
+
+
+def gelu_both(hidden):
+    square = hidden * hidden
+    tangent = jnp.tanh(hidden * (gelu_coef + gelu_coef * 0.044715 * square))
+    half = 0.5 + 0.5 * tangent
+    value = hidden * half
+    slope = half + value * (1.0 - tangent) * (gelu_coef + 3.0 * 0.044715 * gelu_coef * square)
     return (value, slope)
 
 
@@ -137,6 +146,12 @@
     norm_parts,
     line_parts,
     final,
+    up_near,
+    up_middle,
+    up_far,
+    down_near,
+    down_middle,
+    down_far,
     local_sem,
     tok_send,
     tok_recv,
@@ -152,6 +167,8 @@
     final_recv,
 ):
     all_augs, clip_norm = scale_of
+    up_t = (up_near, up_middle, up_far)
+    down_t = (down_near, down_middle, down_far)
     dp = lax.axis_index("dp")
     core = lax.axis_index("aug")
     plane = SIDE * SIDE
@@ -160,6 +177,8 @@
     y = (dp // SIDE) % SIDE
     x = dp % SIDE
     rows = up_in.shape[0]
+    tokens = x_in.shape[0]
+    held = pl.ds(0, tokens)
     block = out.shape[1] // plane
 
     def spot(rel):
@@ -300,28 +319,43 @@
     def inner(slot, which=every):
         pl.when(jnp.logical_not(at_end))(lambda: await_weights(slot, which))
 
+    def two(ref, s):
+        pad = jnp.zeros((u_up.shape[1] - tokens, ref.shape[2]), ref.dtype)
+        return jnp.concatenate([ref[s], pad, ref[s + 1], pad], axis=0)
+
+    def keep(ref, s, value, add=False):
+        value = value.reshape(2, ref.shape[1], ref.shape[2])
+        ref[pl.ds(s, 2)] = ref[pl.ds(s, 2)] + value if add else value
+
     def sides(s):
-        u_up[s] = jnp.dot(xs[s], right_up[...], preferred_element_type=jnp.float32).astype(jnp.bfloat16)
-        v_down[s] = jnp.dot(gs[s], left_down[...], preferred_element_type=jnp.float32).astype(jnp.bfloat16)
-
-    def cell(s, first_slot, slots, fresh):
+        keep(u_up, s, jnp.dot(two(xs, s), right_up[...], preferred_element_type=jnp.float32).astype(jnp.bfloat16))
+        keep(v_down, s, jnp.dot(two(gs, s), left_down[...], preferred_element_type=jnp.float32).astype(jnp.bfloat16))
+
+    groups = {0: 2, 2: 1, 3: line - 3}
+
+    def turn(first_slot):
+        span = pl.ds(first_slot * rows, groups[first_slot] * rows)
+        n = list(groups).index(first_slot)
+        up_t[n][...] = up[span, :].T
+        down_t[n][...] = down[span, :].T
+
+    def cell(s, first_slot, fresh):
+        slots = groups[first_slot]
+        n = list(groups).index(first_slot)
         span = pl.ds(first_slot * rows, slots * rows)
-        hidden = contract_last(xs[s], up[span, :])
-        activation, slope = gelu_pair(hidden)
-        back = contract_last(gs[s], down[span, :])
+        hidden = jnp.dot(two(xs, s), up_t[n][...], preferred_element_type=jnp.float32)
+        activation, slope = gelu_both(hidden)
+        back = jnp.dot(two(gs, s), down_t[n][...], preferred_element_type=jnp.float32)
         hidden_grad = (back * slope).astype(jnp.bfloat16)
         v = jnp.dot(hidden_grad, left[span, :], preferred_element_type=jnp.float32)
         u = jnp.dot(activation.astype(jnp.bfloat16), right[span, :], preferred_element_type=jnp.float32)
-        if fresh:
-            v_acc[s] = v
-            u_acc[s] = u
-        else:
-            v_acc[s] += v
-            u_acc[s] += u
+        keep(v_acc, s, v, not fresh)
+        keep(u_acc, s, u, not fresh)
 
     def over(sets, *steps):
-        @pl.loop(sets[0], sets[1])
-        def _(s):
+        @pl.loop(sets[0] // 2, sets[1] // 2)
+        def _(pair):
+            s = pair * 2
             for step in steps:
                 step(s)
 
@@ -342,7 +376,8 @@
     inner(1, (1, 2, 3))
     inner(2, (1, 2, 3))
     outer(1)
-    near = functools.partial(cell, first_slot=0, slots=2, fresh=True)
+    turn(0)
+    near = functools.partial(cell, first_slot=0, fresh=True)
     over((0, 2), near)
     inner(3, (0,))
     await_token(1, 2)
@@ -360,12 +395,14 @@
     send_token(0, 6, 1)
     await_token(1, 6)
     send_token(1, 6, 1)
-    middle = functools.partial(cell, first_slot=2, slots=1, fresh=False)
+    turn(2)
+    middle = functools.partial(cell, first_slot=2, fresh=False)
     over((0, 6), middle)
     await_token(0, 7)
     await_token(1, 7)
     over((6, 8), sides, near, middle)
     outer(3)
+    turn(3)
 
     def contract_first(a, b):
         return lax.dot_general(a, b, (((0,), (0,)), ((), ())), preferred_element_type=jnp.float32)
@@ -373,10 +410,10 @@
     piece_copies = []
     for i in range(plane):
         first, second = None, None
+        cell(2 * i, 3, False)
         for s in (2 * i, 2 * i + 1):
-            cell(s, 3, line - 3, False)
-            a = contract_first(v_acc[s].astype(jnp.bfloat16), u_up[s])
-            b = contract_first(v_down[s], u_acc[s].astype(jnp.bfloat16))
+            a = contract_first(v_acc[s, held].astype(jnp.bfloat16), u_up[s, held])
+            b = contract_first(v_down[s, held], u_acc[s, held].astype(jnp.bfloat16))
             first = a if first is None else first + a
             second = b if second is None else second + b
         part[i, 0] = first
@@ -492,6 +529,7 @@
     clip_norm = clip_frac * rank * math.sqrt(tokens / all_augs)
     plane = SIDE * SIDE
     members = plane * 2
+    padded = -(-tokens // 16) * 16
     block = noise.shape[1] // plane
     lanes = noise.shape[2]
     bf16, f32 = jnp.bfloat16, jnp.float32
@@ -514,10 +552,10 @@
             pltpu.VMEM(right_up.shape, bf16),
             pltpu.VMEM(left_down.shape, bf16),
             pltpu.VMEM(noise.shape, f32),
-            pltpu.VMEM((members, tokens, rank), f32),
-            pltpu.VMEM((members, tokens, rank), f32),
-            pltpu.VMEM((members, tokens, rank), bf16),
-            pltpu.VMEM((members, tokens, rank), bf16),
+            pltpu.VMEM((members, padded, rank), f32),
+            pltpu.VMEM((members, padded, rank), f32),
+            pltpu.VMEM((members, padded, rank), bf16),
+            pltpu.VMEM((members, padded, rank), bf16),
             pltpu.VMEM((plane, 2, rank, rank), f32),
             pltpu.VMEM((plane, 2, rank, rank), bf16),
             pltpu.VMEM((members - 1, plane, 2, block, lanes), bf16),
@@ -525,6 +563,7 @@
             pltpu.VMEM((members, plane, lanes), f32),
             pltpu.VMEM((line, 2, block, lanes), f32),
             pltpu.VMEM((plane, 2, block, lanes), f32),
+            *[pltpu.VMEM((width, n * rows), bf16) for n in (2, 1, line - 3)] * 2,
             dma((9,)),
             dma((14,)),
             dma((2, members)),

time: 55.6 us -> 53.6 us (0.964)
  Pallas kernels: 52.2 us -> 50.1 us
    pallas_call x1, Pallas kernels: 52.2 us -> 50.1 us  [planes(): pl.pallas_call(functools.partial(kernel, line, all_images, (all_augs, cli...]
where the time goes in v3:
time: 53.6 us; the launch traced here: 53.4 us
  Pallas kernels  50.1 us (93%)
  between operations  1.82 us (3%)
  local copies, waits for them, and re-layouts  1.48 us (3%)
    pallas_call x1, Pallas kernels, planes(): pl.pallas_call(functools.partial(kernel, line, all_images, (all_augs, cli...  50.1 us
    unnamed x3, local copies, waits for them, and re-layouts  1.48 us

profile of v3, /device:TPU:0, one launch (start us, length us, event | category | flops | bytes accessed | tf_op | source)
XLA Modules:
  0.0 53.4 jit_solution(5153055436391690969)
XLA Ops:
  0.6 50.1 %planes.1 = (f32[2,64,128]{2,1,0:T(8,128)}, f32[1,128]{1,0:T(1,128)}) custom-call(bf16[197,768]{1,0:T(8,128)(2,1)} %bitcast.4, bf16[197,768]{1,0:T(8,128)(2,1)} %bitcast.5, bf16[96,768]{1,0:T(8,128)(2,1)} %up_in.1, bf16[96,768]{1,0:T(8,128)(2,1)} %down_in.1, bf16[96,128]{1,0:T(8,128)(2,1)} %left_in.1, bf16[96,128]{1,0:T(8,128)(2,1)} %right_in.1, ...), custom_call_target="tpu_custom_call" | custom-call | tf_op jit(solution)/shard_map/planes/pallas_call | solution.py:537
  50.8 0.0 copy-start
  50.8 1.5 %copy.13 = f32[2,64,128]{2,1,0:T(8,128)} copy(f32[2,64,128]{2,1,0:T(8,128)} %get-tuple-element.8) | data formatting | bytes 131072
  52.3 0.0 copy-done
Async XLA Ops:
  50.8 1.5 %copy-start = (f32[1,128]{1,0:T(1,128)S(1)}, f32[1,128]{1,0:T(1,128)}, u32[]{:S(2)}) copy-start(f32[1,128]{1,0:T(1,128)} %get-tuple-element.5) | copy-start | bytes 1540
